TPU v7x, 32 devices: a whole 2x2x4 slice. The times are simulated.
32 devices in a mesh: parts: 2 (over y), tmpl: 4 (over z), sta: 4 (over x, core).
Axes of the slice: x: 2, y: 2, z: 4, core: 2. Of those that a mesh axis runs over, the one named last changes fastest.
Arguments:
- data: float32 [64, 3, 1280], P(('parts', 'sta'), None, 'tmpl'), parts along dimension 0, as said below
- templates: bfloat16 [32, 3, 16, 256], P('sta', None, 'tmpl'), as said below
- starts: int32 [32, 3, 16], P('sta', None, 'tmpl'), may hold values from 0 to 512
Outputs:
- network: float32 [32, 512], P(('parts', 'tmpl'), 'sta'), parts along dimension 0
There are 2 independent parts, one for each index of `parts`. A program takes and returns all parts, laid end to end along the dimension named above; an argument that names none is the same for every part. Nothing has to cross between parts.
Inputs may be any that keep to these rules, and one draw needn't show every extreme that they name: `data`: finite samples. `templates`: finite samples.
All inputs are finite; a program needn't handle non-finite values.
Results may differ from a plain program's by a relative error of at most 0.0029.
Values sent between devices are 32-bit elements; how exact they have to be, the bound alone decides.
A program may use at most 64 MiB of HBM per device.

v0:
```python
import jax
import jax.numpy as jnp
from jax import lax
from jax.sharding import PartitionSpec as P

TLEN = 256
MAXSHIFT = 512
LAGS = 512
EPS = 1e-06


def window_energy(trace):
    extent = LAGS + MAXSHIFT
    squares = trace * trace
    running = jnp.concatenate([jnp.zeros_like(squares[:, :1]), jnp.cumsum(squares, axis=1)], axis=1)
    return running[:, TLEN : TLEN + extent] - running[:, :extent]


def take_window(row, offset):
    return lax.dynamic_slice_in_dim(row, offset, LAGS, 0)


def local_term(whole, templates, starts):
    extent = LAGS + MAXSHIFT
    stations, channels, samples = whole.shape
    per_group = templates.shape[2]
    groups = stations * channels
    lowered = whole.astype(jnp.bfloat16).reshape(1, groups, samples)
    kernel = templates.reshape(groups * per_group, 1, templates.shape[-1])
    raw = lax.conv_general_dilated(
        lowered,
        kernel,
        (1,),
        "VALID",
        dimension_numbers=("NCH", "OIH", "NCH"),
        feature_group_count=groups,
        preferred_element_type=jnp.float32,
    )[0]
    raw = raw[:, :extent]
    energy = window_energy(whole.reshape(groups, samples))
    energy_rows = jnp.repeat(energy, per_group, axis=0)
    tnorm = jnp.sum(jnp.square(templates.astype(jnp.float32)), axis=-1).reshape(-1)
    offsets = starts.reshape(-1)
    slicer = jax.vmap(take_window)
    aligned = slicer(raw, offsets)
    local = slicer(energy_rows, offsets)
    scale = TLEN * jnp.sqrt((tnorm[:, None] / TLEN + EPS) * (local / TLEN + EPS))
    return jnp.sum((aligned / scale).reshape(groups, per_group, LAGS), axis=0)


def shards(data, templates, starts):
    whole = lax.all_gather(data, "tmpl", axis=2, tiled=True)
    partial_value = local_term(whole, templates, starts)
    summed = lax.psum(partial_value, "sta")
    width = LAGS // lax.axis_size("sta")
    return lax.dynamic_slice_in_dim(summed, lax.axis_index("sta") * width, width, 1)


def solution(mesh):
    return jax.shard_map(
        shards,
        mesh=mesh,
        in_specs=(
            P(("parts", "sta"), None, "tmpl"),
            P("sta", None, "tmpl", None),
            P("sta", None, "tmpl"),
        ),
        out_specs=P(("parts", "tmpl"), "sta"),
        check_vma=False,
    )
```

profile of v0, /device:TPU:0, one launch (start us, length us, event | category | flops | bytes accessed | tf_op | source)
XLA Modules:
  0.0 490.5 jit_solution(16499657202032533554)
XLA Ops:
  1.0 47.9 %all_gather.3 = f32[8,3,1280]{0,1,2:T(4,128)S(1)} all-gather(f32[8,3,320]{0,1,2:T(4,128)S(1)} %copy.29), channel_id=1, replica_groups=mesh['parts'=2,'tmpl'=4,'sta'=4] {'tmpl'}, dimensions={2}, use_global_device_ids=true | all-gather | bytes 153600 | tf_op jit(solution)/shard_map/all_gather | solution.py:52
  49.9 6.8 %reduce-window.6 = f32[24,10,128]{2,1,0:T(8,128)S(1)} reduce-window(f32[24,10,128]{2,1,0:T(8,128)S(1)} %mul.25, f32[]{:T(128)} %constant.9.clone.1), window={size=1x1x128 pad=0_0x0_0x127_0}, to_apply=%region_1.2 | reduce-window | flops 3901440 | bytes 245764 | tf_op jit(solution)/shard_map/reduce-window
  58.0 197.6 %while.3 = (s32[]{:T(128)}, f32[96,1024]{1,0:T(8,128)S(1)}, s32[96,2]{0,1:T(2,128)S(1)}, f32[96,512]{1,0:T(8,128)S(1)}, s32[]{:T(128)}, /*index=5*/s32[]{:T(128)}) while((s32[]{:T(128)}, f32[96,1024]{1,0:T(8,128)S(1)}, s32[96,2]{0,1:T(2,128)S(1)}, f32[96,512]{1,0:T(8,128)S(1)}, s32[]{:T(128)}, /*index=5*/s32[]{:T(128)}) %tuple.38), condition=%wide.while_cond.1, body=%wide.while_body.1.sunk | while | flops 2 | bytes 8305 | solution.py:20
  75.2 1.3 dynamic-slice.15
  77.2 1.3 dynamic-slice.15
  79.3 1.3 dynamic-slice.15
  81.3 1.3 dynamic-slice.15
  83.4 1.3 dynamic-slice.15
  85.5 1.3 dynamic-slice.15
  87.5 1.3 dynamic-slice.15
  89.6 1.3 dynamic-slice.15
  91.6 1.3 dynamic-slice.15
  114.3 1.3 dynamic-slice.15
  116.3 1.3 dynamic-slice.15
  118.4 1.3 dynamic-slice.15
  120.5 1.3 dynamic-slice.15
  122.5 1.3 dynamic-slice.15
  124.6 1.3 dynamic-slice.15
  126.6 1.3 dynamic-slice.15
  128.7 1.3 dynamic-slice.15
  130.7 1.3 dynamic-slice.15
  153.4 1.3 dynamic-slice.15
  155.4 1.3 dynamic-slice.15
  157.5 1.3 dynamic-slice.15
  159.6 1.3 dynamic-slice.15
  161.6 1.3 dynamic-slice.15
  163.7 1.3 dynamic-slice.15
  165.7 1.3 dynamic-slice.15
  167.8 1.3 dynamic-slice.15
  169.9 1.3 dynamic-slice.15
  192.5 1.3 dynamic-slice.15
  194.6 1.3 dynamic-slice.15
  196.6 1.3 dynamic-slice.15
  198.7 1.3 dynamic-slice.15
  200.7 1.3 dynamic-slice.15
  202.8 1.3 dynamic-slice.15
  204.8 1.3 dynamic-slice.15
  206.9 1.3 dynamic-slice.15
  209.0 1.3 dynamic-slice.15
  231.6 1.3 dynamic-slice.15
  233.7 1.3 dynamic-slice.15
  235.7 1.3 dynamic-slice.15
  237.8 1.3 dynamic-slice.15
  239.8 1.3 dynamic-slice.15
  241.9 1.3 dynamic-slice.15
  256.5 28.5 %fusion.1 = f32[1,96,1025]{1,0,2:T(1,128)S(1)} fusion(bf16[1,24,1280]{1,0,2:T(2,128)(2,1)S(1)} %copy.33, s32[96]{0:T(128)S(1)} %copy-done.2, bf16[96,256]{0,1:T(8,128)(2,1)S(1)} %copy.32), kind=kOutput, calls=%fused_computation.4 | convolution fusion | flops 1210318848 | bytes 504576 | tf_op jit(solution)/shard_map/conv_general_dilated | solution.py:30
  285.8 197.6 %while.2 = (s32[]{:T(128)}, f32[96,1024]{1,0:T(8,128)S(1)}, s32[96,2]{0,1:T(2,128)S(1)}, f32[96,512]{1,0:T(8,128)S(1)}, s32[]{:T(128)}, /*index=5*/s32[]{:T(128)}) while((s32[]{:T(128)}, f32[96,1024]{1,0:T(8,128)S(1)}, s32[96,2]{0,1:T(2,128)S(1)}, f32[96,512]{1,0:T(8,128)S(1)}, s32[]{:T(128)}, /*index=5*/s32[]{:T(128)}) %tuple.41), condition=%wide.while_cond, body=%wide.while_body.sunk | while | flops 2 | bytes 8305 | solution.py:20
  484.1 5.8 %psum.7 = f32[4,512]{1,0:T(4,128)S(1)} all-reduce(f32[4,512]{1,0:T(4,128)S(1)} %fusion.5), channel_id=1, replica_groups=mesh['parts'=2,'tmpl'=4,'sta'=4] {'sta'}, use_global_device_ids=true, to_apply=%region_4.5 | all-reduce | flops 2048 | bytes 16384 | tf_op jit(solution)/shard_map/psum | solution.py:54
  (770 shorter events, 340.9 us)
Async XLA Ops:
  56.7 1.0 copy-start.1
  57.6 198.7 %copy-start = (bf16[8,3,4,256]{3,2,1,0:T(4,128)(2,1)S(1)}, bf16[8,3,4,256]{3,2,1,0:T(4,128)(2,1)}, u32[]{:S(2)}) copy-start(bf16[8,3,4,256]{3,2,1,0:T(4,128)(2,1)} %param.4) | copy-start | bytes 147460
  57.6 198.9 %copy-start.2 = (s32[96]{0:T(128)S(1)}, s32[96]{0:T(128)}, u32[]{:S(2)}) copy-start(s32[96]{0:T(128)} %constant.11.clone.1) | copy-start | bytes 1156
where the time goes:
time: 494 us; the launch traced here: 490 us
  local copies, waits for them, and re-layouts  396 us (80%)
  blocking collectives  53.7 us (11%)
  matrix products  28.5 us (6%)
  other arithmetic  7.52 us (2%)
    gather x768, local copies, waits for them, and re-layouts  391 us
    all_gather x1, blocking collectives, shards(): whole = lax.all_gather(data, 'tmpl', axis=2, tiled=True)  47.9 us
    conv_general_dilated x1, matrix products, local_term(): lax.conv_general_dilated(lowered, kernel, (1,), 'VALID', dimension_number...  28.5 us

commit v1 on v0

--- a/solution.py
+++ b/solution.py
@@ -49,7 +49,14 @@
 
 
 def shards(data, templates, starts):
-    whole = lax.all_gather(data, "tmpl", axis=2, tiled=True)
+    ways = lax.axis_size("tmpl")
+    pieces = [data]
+    for far in range(1, ways):
+        pieces.append(
+            lax.ppermute(pieces[far - 1], "tmpl", [(d, (d - 1) % ways) for d in range(ways)])
+        )
+    line = jnp.concatenate(pieces, axis=2)
+    whole = jnp.roll(line, lax.axis_index("tmpl") * data.shape[2], axis=2)
     partial_value = local_term(whole, templates, starts)
     summed = lax.psum(partial_value, "sta")
     width = LAGS // lax.axis_size("sta")

time: 494 us -> 463 us (0.937)
  blocking collectives: 53.7 us -> 5.77 us
  starting transfers between devices: 0 us -> 13.2 us
    all_gather x1 -> x0, blocking collectives: 47.9 us -> none  [shards(): whole = lax.all_gather(data, 'tmpl', axis=2, tiled=True)]
    ppermute x0 -> x3, starting transfers between devices: none -> 13.2 us  [shards(): lax.ppermute(pieces[far - 1], 'tmpl', [(d, (d - 1) % ways) for d in range...]
  transfers between devices with their start and end apart: 0 -> 3, of which waited for: 0 -> 2; matrix products, arithmetic and copies ran while one was open for 0% -> 1% of each run, Pallas kernels for 0% -> 0%
where the time goes in v1:
time: 463 us; the launch traced here: 460 us
  local copies, waits for them, and re-layouts  397 us (86%)
  matrix products  28.5 us (6%)
  starting transfers between devices  13.2 us (3%)
  other arithmetic  8.38 us (2%)
  blocking collectives  5.77 us (1%)
  loops' own time  4.65 us (1%)
    gather x768, local copies, waits for them, and re-layouts  391 us
    conv_general_dilated x1, matrix products, local_term(): lax.conv_general_dilated(lowered, kernel, (1,), 'VALID', dimension_number...  28.5 us
    ppermute x3, starting transfers between devices, shards(): lax.ppermute(pieces[far - 1], 'tmpl', [(d, (d - 1) % ways) for d in range...  13.2 us
  transfers between devices with their start and end apart: 3, of which 2 were waited for; matrix products, arithmetic and copies ran while one was open for 1% of the time, Pallas kernels for 0%

profile of v1, /device:TPU:0, one launch (start us, length us, event | category | flops | bytes accessed | tf_op | source)
XLA Modules:
  0.0 459.5 jit_solution(16802766882999763056)
XLA Ops:
  0.0 5.0 %collective-permute-start = (f32[8,3,320]{2,0,1:T(8,128)}, f32[8,3,320]{2,0,1:T(8,128)S(1)}, u32[]{:S(2)}, u32[]{:S(2)}) collective-permute-start(f32[8,3,320]{2,0,1:T(8,128)} %param.3), channel_id=1, source_target_pairs={{0,12},{4,0},{8,4},{12,8},{1,13},{5,1},{9,5},{13,9},{2,14},{6,2},{... | collective-permute-start | bytes 92168 | tf_op jit(solution)/shard_map/ppermute | solution.py:56
  7.0 4.0 collective-permute-start.1
  11.0 1.6 collective-permute-done.1
  12.7 4.1 collective-permute-start.2
  19.8 6.8 %reduce-window.6 = f32[24,10,128]{2,1,0:T(8,128)S(1)} reduce-window(f32[24,10,128]{2,1,0:T(8,128)S(1)} %mul.29, f32[]{:T(128)} %constant.50.clone.1), window={size=1x1x128 pad=0_0x0_0x127_0}, to_apply=%region_1.2 | reduce-window | flops 3901440 | bytes 245764 | tf_op jit(solution)/shard_map/reduce-window
  27.6 197.6 %while.3 = (s32[]{:T(128)}, f32[96,1024]{1,0:T(8,128)S(1)}, s32[96,2]{0,1:T(2,128)S(1)}, f32[96,512]{1,0:T(8,128)S(1)}, s32[]{:T(128)}, /*index=5*/s32[]{:T(128)}) while((s32[]{:T(128)}, f32[96,1024]{1,0:T(8,128)S(1)}, s32[96,2]{0,1:T(2,128)S(1)}, f32[96,512]{1,0:T(8,128)S(1)}, s32[]{:T(128)}, /*index=5*/s32[]{:T(128)}) %tuple.37), condition=%wide.while_cond.1, body=%wide.while_body.1.sunk | while | flops 2 | bytes 8305 | solution.py:20
  48.8 1.3 dynamic-slice.15
  50.9 1.3 dynamic-slice.15
  52.9 1.3 dynamic-slice.15
  55.0 1.3 dynamic-slice.15
  57.1 1.3 dynamic-slice.15
  59.1 1.3 dynamic-slice.15
  61.2 1.3 dynamic-slice.15
  63.2 1.3 dynamic-slice.15
  65.3 1.3 dynamic-slice.15
  87.9 1.3 dynamic-slice.15
  90.0 1.3 dynamic-slice.15
  92.1 1.3 dynamic-slice.15
  94.1 1.3 dynamic-slice.15
  96.2 1.3 dynamic-slice.15
  98.2 1.3 dynamic-slice.15
  100.3 1.3 dynamic-slice.15
  102.3 1.3 dynamic-slice.15
  104.4 1.3 dynamic-slice.15
  127.0 1.3 dynamic-slice.15
  129.1 1.3 dynamic-slice.15
  131.2 1.3 dynamic-slice.15
  133.2 1.3 dynamic-slice.15
  135.3 1.3 dynamic-slice.15
  137.3 1.3 dynamic-slice.15
  139.4 1.3 dynamic-slice.15
  141.5 1.3 dynamic-slice.15
  143.5 1.3 dynamic-slice.15
  166.2 1.3 dynamic-slice.15
  168.2 1.3 dynamic-slice.15
  170.3 1.3 dynamic-slice.15
  172.3 1.3 dynamic-slice.15
  174.4 1.3 dynamic-slice.15
  176.5 1.3 dynamic-slice.15
  178.5 1.3 dynamic-slice.15
  180.6 1.3 dynamic-slice.15
  182.6 1.3 dynamic-slice.15
  205.3 1.3 dynamic-slice.15
  207.3 1.3 dynamic-slice.15
  209.4 1.3 dynamic-slice.15
  225.9 28.5 %fusion.1 = f32[1,96,1025]{1,0,2:T(1,128)S(1)} fusion(bf16[1,24,1280]{1,0,2:T(2,128)(2,1)S(1)} %copy.30, s32[96]{0:T(128)S(1)} %copy-done, bf16[96,256]{0,1:T(8,128)(2,1)S(1)} %copy.29), kind=kOutput, calls=%fused_computation.4 | convolution fusion | flops 1210318848 | bytes 504576 | tf_op jit(solution)/shard_map/conv_general_dilated | solution.py:30
  255.2 197.6 %while.2 = (s32[]{:T(128)}, f32[96,1024]{1,0:T(8,128)S(1)}, s32[96,2]{0,1:T(2,128)S(1)}, f32[96,512]{1,0:T(8,128)S(1)}, s32[]{:T(128)}, /*index=5*/s32[]{:T(128)}) while((s32[]{:T(128)}, f32[96,1024]{1,0:T(8,128)S(1)}, s32[96,2]{0,1:T(2,128)S(1)}, f32[96,512]{1,0:T(8,128)S(1)}, s32[]{:T(128)}, /*index=5*/s32[]{:T(128)}) %tuple.40), condition=%wide.while_cond, body=%wide.while_body.sunk | while | flops 2 | bytes 8305 | solution.py:20
  453.2 5.8 %psum.7 = f32[4,512]{1,0:T(4,128)S(1)} all-reduce(f32[4,512]{1,0:T(4,128)S(1)} %fusion.5), channel_id=1, replica_groups=mesh['parts'=2,'tmpl'=4,'sta'=4] {'sta'}, use_global_device_ids=true, to_apply=%region_4.5 | all-reduce | flops 2048 | bytes 16384 | tf_op jit(solution)/shard_map/psum | solution.py:61
  (771 shorter events, 347.1 us)
Async XLA Ops:
  0.0 7.0 %collective-permute-start = (f32[8,3,320]{2,0,1:T(8,128)}, f32[8,3,320]{2,0,1:T(8,128)S(1)}, u32[]{:S(2)}, u32[]{:S(2)}) collective-permute-start(f32[8,3,320]{2,0,1:T(8,128)} %param.3), channel_id=1, source_target_pairs={{0,12},{4,0},{8,4},{12,8},{1,13},{5,1},{9,5},{13,9},{2,14},{6,2},{... | collective-permute-start | bytes 92168 | tf_op jit(solution)/shard_map/ppermute | solution.py:56
  7.0 5.7 %collective-permute-start.1 = (f32[8,3,320]{2,0,1:T(8,128)S(1)}, f32[8,3,320]{2,0,1:T(8,128)S(1)}, u32[]{:S(2)}, u32[]{:S(2)}) collective-permute-start(f32[8,3,320]{2,0,1:T(8,128)S(1)} %collective-permute-done), channel_id=1, source_target_pairs={{0,12},{4,0},{8,4},{12,8},{1,13},{5,1},{9,5},{13,9},{2,14},{6,2},{... | collective-permute-start | bytes 92168 | tf_op jit(solution)/shard_map/ppermute | solution.py:56
  12.7 5.8 %collective-permute-start.2 = (f32[8,3,320]{2,0,1:T(8,128)S(1)}, f32[8,3,320]{2,0,1:T(8,128)S(1)}, u32[]{:S(2)}, u32[]{:S(2)}) collective-permute-start(f32[8,3,320]{2,0,1:T(8,128)S(1)} %collective-permute-done.1), channel_id=1, source_target_pairs={{0,12},{4,0},{8,4},{12,8},{1,13},{5,1},{9,5},{13,9},{2,14},{6,2},{... | collective-permute-start | bytes 92168 | tf_op jit(solution)/shard_map/ppermute | solution.py:56
  225.2 0.7 copy-start
